TPU v7x, 256 devices: a whole 4x4x8 slice. The times are simulated.
256 devices in a mesh: tp: 8 (over x, core), ad: 32 (over y, z).
Axes of the slice: x: 4, y: 4, z: 8, core: 2. Of those that a mesh axis runs over, the one named last changes fastest.
Arguments:
- hidden: bfloat16 [14336, 8192], P('ad'), may hold values from -6 to 6
- gain: bfloat16 [8192], replicated, may hold values from 0.25 to 1.75
- key_value_weight: bfloat16 [8192, 2, 1024], P(None, None, 'tp'), may hold values from -0.0625 to 0.0625
- adapter_down_weight: bfloat16 [64, 8192, 128], P('ad', 'tp'), may hold values from -0.0625 to 0.0625
- adapter_up_weight: bfloat16 [64, 2, 64, 1024], P('ad', None, None, 'tp'), may hold values from -0.75 to 0.75
- language_pair_index: int32 [14336], P('ad'), may hold values from 0 to 63, as said below
- adapter_row_index: int32 [64], replicated, may hold values from 0 to 63, as said below
Outputs:
- kv_out: bfloat16 [14336, 2, 1024], P('ad', None, 'tp')
Inputs may be any that keep to these rules, and one draw needn't show every extreme that they name: A row's owner is adapter_row_index[language_pair_index] // 2. Among the rows of one device, one owner, the same for every device, has exactly 56 rows; every other owner has at most 28, and one other owner, the same for every device, exactly 28. `adapter_row_index`: each adapter's row in adapter_down_weight and adapter_up_weight; every row appears once.
All inputs are finite; a program needn't handle non-finite values.
Results may differ from a plain program's by a relative error of at most 0.0053.
Values may be sent and summed in bfloat16 or wider, within the bound.
No kernel may reach another device: no remote copies, remote signals or barrier semaphores. Data moves between devices by JAX's collectives and lax.ppermute only.
A program may use at most 128 MiB of HBM per device.

v0:
```python
import jax
import jax.numpy as jnp
from jax import lax
from jax.sharding import PartitionSpec as P

epsilon = 1e-05
adapter_scale = 0.5


def down_local(rows_in, row_ids, down_table):
    adapter_total = down_table.shape[0]
    labels = jnp.arange(adapter_total, dtype=jnp.int32)
    row_mask = row_ids[:, None] == labels[None, :]
    every_low = jnp.einsum("rc,acm->ram", rows_in, down_table, preferred_element_type=jnp.float32)
    partial_low = jnp.sum(jnp.where(row_mask[:, :, None], every_low, jnp.float32(0.0)), axis=1)
    return (partial_low, row_mask)


def upward_delta(summed_low, row_mask, up_table):
    narrow = summed_low.astype(jnp.bfloat16)
    row_total = narrow.shape[0]
    adapter_total = up_table.shape[0]
    rank_width = up_table.shape[2]
    widened = jnp.where(row_mask[:, :, None], narrow[:, None, :], jnp.zeros((), jnp.bfloat16))
    widened = widened.reshape(row_total, adapter_total, 2, rank_width)
    values = jnp.einsum("racq,acqh->rch", widened, up_table, preferred_element_type=jnp.float32)
    return values.astype(jnp.bfloat16)


def on_device(
    hidden,
    gain,
    key_value_weight,
    adapter_down_weight,
    adapter_up_weight,
    language_pair_index,
    adapter_row_index,
):
    tok_count = hidden.shape[0]
    model_width = hidden.shape[1]
    owner_count = lax.axis_size("ad")
    by_holder = adapter_down_weight.shape[0]
    column_portion = adapter_down_weight.shape[1]
    head_cols = key_value_weight.shape[2]
    row_quota = tok_count // owner_count
    wide_hidden = hidden.astype(jnp.float32)
    inv_rms = lax.rsqrt(jnp.mean(wide_hidden * wide_hidden, axis=-1, keepdims=True) + epsilon)
    normed = (wide_hidden * inv_rms * gain.astype(jnp.float32)).astype(jnp.bfloat16)
    base_projection = jnp.dot(
        normed,
        key_value_weight.reshape(model_width, 2 * head_cols),
        preferred_element_type=jnp.float32,
    ).reshape(tok_count, 2, head_cols)
    own_cols = lax.dynamic_slice_in_dim(
        normed, lax.axis_index("tp") * column_portion, column_portion, 1
    )
    slot_ids = adapter_row_index[language_pair_index]
    owner_ids = slot_ids // by_holder
    local_ids = slot_ids % by_holder
    owner_labels = jnp.arange(owner_count, dtype=jnp.int32)
    capacity = 4 * row_quota
    onehot = (owner_ids[:, None] == owner_labels[None, :]).astype(jnp.int32)
    before = jnp.cumsum(onehot, axis=0) - onehot
    bucket_pos = jnp.sum(before * onehot, axis=1)
    total_slots = owner_count * capacity
    dest_slot = jnp.where(owner_ids < owner_count, owner_ids * capacity + bucket_pos, total_slots)
    slot_labels = jnp.arange(total_slots, dtype=jnp.int32)
    selector = slot_labels[:, None] == dest_slot[None, :]
    selector_bf = selector.astype(jnp.bfloat16)
    send_rows = jnp.dot(selector_bf, own_cols, preferred_element_type=jnp.float32).astype(
        jnp.bfloat16
    )
    send_rows = send_rows.reshape(owner_count, capacity, column_portion)
    filled = jnp.any(selector, axis=1)
    picked_ids = jnp.sum(jnp.where(selector, local_ids[None, :], 0), axis=1)
    send_ids = jnp.where(filled, picked_ids, by_holder).reshape(owner_count, capacity)
    received_rows = lax.all_to_all(send_rows, "ad", split_axis=0, concat_axis=0, tiled=True)
    got_ids = lax.all_to_all(send_ids, "ad", split_axis=0, concat_axis=0, tiled=True)
    source_count = got_ids.shape[0]
    element_count = got_ids.shape[1]
    flat_ids = got_ids.reshape(source_count * element_count)
    partial_low, row_mask = down_local(
        received_rows.reshape(source_count * element_count, column_portion),
        flat_ids,
        adapter_down_weight,
    )
    summed_output = lax.psum(partial_low, "tp")
    delta_rows = upward_delta(summed_output, row_mask, adapter_up_weight).reshape(
        source_count, element_count, 2, head_cols
    )
    returned = lax.all_to_all(delta_rows, "ad", split_axis=0, concat_axis=0, tiled=True)
    flat_back = returned.reshape(total_slots, 2 * head_cols)
    back_rows = jnp.einsum("st,sc->tc", selector_bf, flat_back, preferred_element_type=jnp.float32)
    delta_by_row = back_rows.astype(jnp.bfloat16).reshape(tok_count, 2, head_cols)
    return (base_projection + adapter_scale * delta_by_row.astype(jnp.float32)).astype(jnp.bfloat16)


def solution(mesh):
    return jax.shard_map(
        on_device,
        mesh=mesh,
        in_specs=(
            P("ad", None),
            P(),
            P(None, None, "tp"),
            P("ad", "tp", None),
            P("ad", None, None, "tp"),
            P("ad"),
            P(),
        ),
        out_specs=P("ad", None, "tp"),
        check_vma=False,
    )
```

profile of v0, /device:TPU:6, one launch (start us, length us, event | category | flops | bytes accessed | tf_op | source)
XLA Modules:
  0.0 251.6 jit_solution(11058479754245148850)
XLA Ops:
  0.0 0.0 copy-start
  0.0 2.1 fusion.34
  2.1 2.1 fusion.35
  4.1 2.1 fusion.36
  6.2 1.6 fusion.37
  7.8 40.5 %add_select_fusion = (s32[448]{0:T(512)S(1)}, s32[448]{0:T(512)S(1)}) fusion(s32[]{:T(128)} %bitcast.66, s32[]{:T(128)} %bitcast.65, s32[]{:T(128)} %bitcast.64, s32[]{:T(128)} %bitcast.63, s32[]{:T(128)} %bitcast.62, s32[]{:T(128)} %bitcast.61, s32[]{:T(128)} %bitcast.60, s32[]{:T(128)} %bitcast.59, s32[]{:T(128)} %bitcast.58, s32[]{:T(128)} %bitcast.57, ...), kind=kLoop, calls=%fused_computation.46 | loop fusion | flops 62720 | bytes 5632 | tf_op jit(solution)/shard_map/jit(remainder)/select_n | solution.py:59
  48.4 1.2 reduce-window.6
  49.6 0.2 slice_reduce_fusion
  49.8 0.1 bitcast_bitcast_fusion.1
  50.0 0.6 fusion.6
  50.5 0.4 select_reduce_fusion
  51.0 0.7 select_n.72
  51.7 11.5 %all-to-all-start = ((s32[32,1,56]{2,1,0:T(1,128)}), s32[32,1,56]{2,1,0:T(1,128)S(1)}, u32[]{:S(2)}, u32[]{:S(2)}) async-start(s32[32,1,56]{2,1,0:T(1,128)} %select_n.72), calls=%async_computation | async-start | bytes 32768 | tf_op jit(solution)/shard_map/all_to_all | solution.py:78
  63.2 0.7 convert_element_type.37
  63.9 4.6 %fusion = f32[448]{0:T(512)S(1)} fusion(bf16[448,8192]{1,0:T(8,128)(2,1)} %param.7), kind=kLoop, calls=%fused_computation.2 | loop fusion | flops 11009600 | bytes 7341824 | tf_op jit(solution)/shard_map/reduce_sum | solution.py:47
  68.5 5.5 %fusion.2 = bf16[448,8192]{1,0:T(8,128)(2,1)S(1)} fusion(bf16[448,8192]{1,0:T(8,128)(2,1)} %param.7, f32[8192]{0:T(1024)S(1)} %convert_element_type.37, f32[448]{0:T(512)S(1)} %add_rsqrt_fusion), kind=kLoop, calls=%fused_computation.4 | loop fusion | flops 14680064 | bytes 14714624 | tf_op jit(solution)/shard_map/convert_element_type | solution.py:48
  74.1 0.0 copy-start.1
  74.1 3.0 %copy-done.1 = bf16[448,8192]{1,0:T(8,128)(2,1)} copy-done((bf16[448,8192]{1,0:T(8,128)(2,1)}, bf16[448,8192]{1,0:T(8,128)(2,1)S(1)}, u32[]{:S(2)}) %copy-start.1) | copy-done | bytes 7340056
  77.0 4.1 %convolution_convert_fusion = bf16[1792,1024]{1,0:T(8,128)(2,1)} fusion(s32[448]{0:T(512)S(1)} %add_select_fusion.2, bf16[448,8192]{1,0:T(8,128)(2,1)S(1)} %fusion.2, s32[]{:T(128)S(6)} %select_n.73), kind=kOutput, calls=%fused_computation.8 | convolution fusion | flops 1646804992 | bytes 4589572 | tf_op jit(solution)/shard_map/dot_general | solution.py:70
  81.2 0.0 all-to-all-done
  81.2 9.9 %all-to-all-start.1 = ((bf16[32,56,1024]{2,1,0:T(8,128)(2,1)}), bf16[32,56,1024]{2,1,0:T(8,128)(2,1)}, u32[]{:S(2)}, u32[]{:S(2)}) async-start(bf16[32,56,1024]{2,1,0:T(8,128)(2,1)} %bitcast.119), calls=%async_computation.1 | async-start | bytes 7340032 | tf_op jit(solution)/shard_map/all_to_all | solution.py:77
  91.1 0.5 broadcast.414
  91.6 0.7 reduce.5
  92.3 0.1 eq.63
  92.4 84.1 %all-to-all-done.1 = bf16[32,56,1024]{2,1,0:T(8,128)(2,1)} async-done(((bf16[32,56,1024]{2,1,0:T(8,128)(2,1)}), bf16[32,56,1024]{2,1,0:T(8,128)(2,1)}, u32[]{:S(2)}, u32[]{:S(2)}) %all-to-all-start.1) | async-done | bytes 3670048 | tf_op jit(solution)/shard_map/all_to_all | solution.py:77
  176.5 0.0 copy-done
  176.5 0.0 copy-start.2
  176.5 3.2 %fusion.10 = f32[1792,128]{1,0:T(8,128)S(1)} fusion(bf16[1792,1024,1]{1,0,2:T(8,128)(2,1)} %bitcast.70, bf16[2,1024,128]{2,1,0:T(8,128)(2,1)S(1)} %copy-done, pred[1792,2]{0,1:T(4,128)(4,1)S(1)} %iota_compare_fusion.13), kind=kOutput, calls=%fused_computation.18 | convolution fusion | flops 940212224 | bytes 5115392 | tf_op jit(solution)/shard_map/rc,acm->ram/dot_general | solution.py:14
  179.7 28.7 %all-reduce.2 = bf16[1792,128]{1,0:T(8,128)(2,1)S(1)} all-reduce(f32[1792,128]{1,0:T(8,128)S(1)} %fusion.10), channel_id=1, replica_groups=mesh['tp'=8,'ad'=32] {'tp'}, use_global_device_ids=true, to_apply=%region_7.8 | all-reduce | flops 229376 | bytes 1376256 | tf_op jit(solution)/shard_map/psum | solution.py:87
  208.4 0.2 copy.37
  208.6 0.0 copy-done.2
  208.6 0.5 fusion.7
  209.1 1.9 copy.39
  211.0 6.2 %all-to-all-start.2 = ((bf16[32,56,2,128]{3,2,1,0:T(2,128)(2,1)}), bf16[32,56,2,128]{3,2,1,0:T(2,128)(2,1)S(1)}, u32[]{:S(2)}, u32[]{:S(2)}) async-start(bf16[32,56,2,128]{3,2,1,0:T(2,128)(2,1)} %copy.39), calls=%async_computation.2 | async-start | bytes 1835008 | tf_op jit(solution)/shard_map/all_to_all | solution.py:91
  217.2 4.8 %copy.58 = bf16[1024,8,2,128]{3,1,2,0:T(8,128)(2,1)} copy(bf16[1024,8,2,128]{3,2,1,0:T(2,128)(2,1)} %bitcast.117) | data formatting | bytes 8388608
  222.0 6.4 %copy.34 = bf16[256,8192]{1,0:T(8,128)(2,1)} copy(bf16[256,8192]{0,1:T(8,128)(2,1)} %bitcast.116) | data formatting | bytes 8388608 | tf_op jit(solution)/shard_map/dot_general | solution.py:49
  228.4 15.2 %all-to-all-done.2 = bf16[32,56,2,128]{3,2,1,0:T(2,128)(2,1)S(1)} async-done(((bf16[32,56,2,128]{3,2,1,0:T(2,128)(2,1)}), bf16[32,56,2,128]{3,2,1,0:T(2,128)(2,1)S(1)}, u32[]{:S(2)}, u32[]{:S(2)}) %all-to-all-start.2) | async-done | bytes 917536 | tf_op jit(solution)/shard_map/all_to_all | solution.py:91
  243.5 0.7 fusion.17
  244.3 6.4 %fusion.18 = bf16[448,2,128]{2,0,1:T(8,128)(2,1)S(1)} fusion(bf16[2,128,8192]{2,1,0:T(8,128)(2,1)} %bitcast.118, bf16[448,8192]{1,0:T(8,128)(2,1)} %copy-done.1, f32[56,2,8,128]{3,2,1,0:T(8,128)S(1)} %fusion.17), kind=kOutput, calls=%fused_computation.24 | convolution fusion | flops 1879277568 | bytes 12222464 | tf_op jit(solution)/shard_map/dot_general | solution.py:49
  250.7 0.9 copy.41
  (10 shorter events, 0.1 us)
Async XLA Ops:
  0.0 176.5 %copy-start = (bf16[2,1024,128]{2,1,0:T(8,128)(2,1)S(1)}, bf16[2,1024,128]{2,1,0:T(8,128)(2,1)}, u32[]{:S(2)}) copy-start(bf16[2,1024,128]{2,1,0:T(8,128)(2,1)} %param.10) | copy-start | bytes 1572868
  51.7 29.5 %all-to-all-start = ((s32[32,1,56]{2,1,0:T(1,128)}), s32[32,1,56]{2,1,0:T(1,128)S(1)}, u32[]{:S(2)}, u32[]{:S(2)}) async-start(s32[32,1,56]{2,1,0:T(1,128)} %select_n.72), calls=%async_computation | async-start | bytes 32768 | tf_op jit(solution)/shard_map/all_to_all | solution.py:78
  74.1 3.0 %copy-start.1 = (bf16[448,8192]{1,0:T(8,128)(2,1)}, bf16[448,8192]{1,0:T(8,128)(2,1)S(1)}, u32[]{:S(2)}) copy-start(bf16[448,8192]{1,0:T(8,128)(2,1)S(1)} %fusion.2) | copy-start | bytes 22020100
  81.2 95.3 %all-to-all-start.1 = ((bf16[32,56,1024]{2,1,0:T(8,128)(2,1)}), bf16[32,56,1024]{2,1,0:T(8,128)(2,1)}, u32[]{:S(2)}, u32[]{:S(2)}) async-start(bf16[32,56,1024]{2,1,0:T(8,128)(2,1)} %bitcast.119), calls=%async_computation.1 | async-start | bytes 7340032 | tf_op jit(solution)/shard_map/all_to_all | solution.py:77
  176.5 32.1 %copy-start.2 = (bf16[2,2,64,128]{3,2,1,0:T(8,128)(2,1)S(1)}, bf16[2,2,64,128]{3,2,1,0:T(8,128)(2,1)}, u32[]{:S(2)}) copy-start(bf16[2,2,64,128]{3,2,1,0:T(8,128)(2,1)} %param.11) | copy-start | bytes 196612
  211.0 32.6 %all-to-all-start.2 = ((bf16[32,56,2,128]{3,2,1,0:T(2,128)(2,1)}), bf16[32,56,2,128]{3,2,1,0:T(2,128)(2,1)S(1)}, u32[]{:S(2)}, u32[]{:S(2)}) async-start(bf16[32,56,2,128]{3,2,1,0:T(2,128)(2,1)} %copy.39), calls=%async_computation.2 | async-start | bytes 1835008 | tf_op jit(solution)/shard_map/all_to_all | solution.py:91
where the time goes:
time: 253 us; the launch traced here: 252 us
  waiting for transfers between devices  99.2 us (39%)
  other arithmetic  54.5 us (22%)
  blocking collectives  28.7 us (11%)
  starting transfers between devices  27.6 us (11%)
  local copies, waits for them, and re-layouts  26.5 us (10%)
  matrix products  14.9 us (6%)
    all_to_all x1, waiting for transfers between devices, on_device(): lax.all_to_all(send_rows, 'ad', split_axis=0, concat_axis=0, tiled=True)  84.1 us
    select_n x1, other arithmetic, on_device(): local_ids = slot_ids % by_holder  40.5 us
    psum x1, blocking collectives, on_device(): summed_output = lax.psum(partial_low, 'tp')  28.7 us
    all_to_all x1, waiting for transfers between devices, on_device(): lax.all_to_all(delta_rows, 'ad', split_axis=0, concat_axis=0, tiled=True)  15.2 us
    all_to_all x1, starting transfers between devices, on_device(): lax.all_to_all(send_ids, 'ad', split_axis=0, concat_axis=0, tiled=True)  11.5 us
    all_to_all x1, starting transfers between devices, on_device(): lax.all_to_all(send_rows, 'ad', split_axis=0, concat_axis=0, tiled=True)  9.9 us
    gather x4, local copies, waits for them, and re-layouts, on_device(): slot_ids = adapter_row_index[language_pair_index]  7.79 us
    unnamed x7, local copies, waits for them, and re-layouts  7.74 us
  transfers between devices with their start and end apart: 3, of which 2 were waited for; matrix products, arithmetic and copies ran while one was open for 11% of the time, Pallas kernels for 0%

commit v1 on v0

--- a/solution.py
+++ b/solution.py
@@ -84,7 +84,7 @@
         flat_ids,
         adapter_down_weight,
     )
-    summed_output = lax.psum(partial_low, "tp")
+    summed_output = jnp.sum(lax.all_gather(partial_low, "tp"), axis=0)
     delta_rows = upward_delta(summed_output, row_mask, adapter_up_weight).reshape(
         source_count, element_count, 2, head_cols
     )

time: 253 us -> 291 us (1.15)
  waiting for transfers between devices: 99.2 us -> 143 us
  blocking collectives: 28.7 us -> 0 us
  between operations: 0.2 us -> 13.6 us
  starting transfers between devices: 27.6 us -> 31.5 us
  other arithmetic: 54.5 us -> 58 us
    all_gather x0 -> x1, waiting for transfers between devices: none -> 43.7 us  [on_device(): summed_output = jnp.sum(lax.all_gather(partial_low, 'tp'), axis=0)]
    psum x1 -> x0, blocking collectives: 28.7 us -> none  [on_device(): summed_output = lax.psum(partial_low, 'tp')]
    all_to_all x1, starting transfers between devices: 6.24 us -> 9.94 us  [on_device(): lax.all_to_all(delta_rows, 'ad', split_axis=0, concat_axis=0, tiled=True)]
    reduce_sum x0 -> x1, other arithmetic: none -> 3.51 us  [on_device(): summed_output = jnp.sum(lax.all_gather(partial_low, 'tp'), axis=0)]
  transfers between devices with their start and end apart: 3 -> 4, of which waited for: 2 -> 3; matrix products, arithmetic and copies ran while one was open for 11% -> 10% of each run, Pallas kernels for 0% -> 0%
where the time goes in v1:
time: 291 us; the launch traced here: 288 us
  waiting for transfers between devices  143 us (49%)
  other arithmetic  58 us (20%)
  starting transfers between devices  31.5 us (11%)
  local copies, waits for them, and re-layouts  26.5 us (9%)
  matrix products  15.9 us (5%)
  between operations  13.6 us (5%)
    all_to_all x1, waiting for transfers between devices, on_device(): lax.all_to_all(send_rows, 'ad', split_axis=0, concat_axis=0, tiled=True)  83.8 us
    all_gather x1, waiting for transfers between devices, on_device(): summed_output = jnp.sum(lax.all_gather(partial_low, 'tp'), axis=0)  43.7 us
    select_n x1, other arithmetic, on_device(): local_ids = slot_ids % by_holder  40.5 us
    all_to_all x1, waiting for transfers between devices, on_device(): lax.all_to_all(delta_rows, 'ad', split_axis=0, concat_axis=0, tiled=True)  15.1 us
    all_to_all x1, starting transfers between devices, on_device(): lax.all_to_all(send_ids, 'ad', split_axis=0, concat_axis=0, tiled=True)  11.5 us
    all_to_all x1, starting transfers between devices, on_device(): lax.all_to_all(delta_rows, 'ad', split_axis=0, concat_axis=0, tiled=True)  9.94 us
    all_to_all x1, starting transfers between devices, on_device(): lax.all_to_all(send_rows, 'ad', split_axis=0, concat_axis=0, tiled=True)  9.9 us
    gather x4, local copies, waits for them, and re-layouts, on_device(): slot_ids = adapter_row_index[language_pair_index]  7.79 us
  transfers between devices with their start and end apart: 4, of which 3 were waited for; matrix products, arithmetic and copies ran while one was open for 10% of the time, Pallas kernels for 0%

profile of v1, /device:TPU:6, one launch (start us, length us, event | category | flops | bytes accessed | tf_op | source)
XLA Modules:
  0.0 288.1 jit_solution(17785102270740880417)
XLA Ops:
  6.5 0.0 copy-start
  6.5 2.1 fusion.34
  8.6 2.1 fusion.35
  10.7 2.1 fusion.36
  12.8 1.6 fusion.37
  14.3 40.5 %add_select_fusion = (s32[448]{0:T(512)S(1)}, s32[448]{0:T(512)S(1)}) fusion(s32[]{:T(128)} %bitcast.66, s32[]{:T(128)} %bitcast.65, s32[]{:T(128)} %bitcast.64, s32[]{:T(128)} %bitcast.63, s32[]{:T(128)} %bitcast.62, s32[]{:T(128)} %bitcast.61, s32[]{:T(128)} %bitcast.60, s32[]{:T(128)} %bitcast.59, s32[]{:T(128)} %bitcast.58, s32[]{:T(128)} %bitcast.57, ...), kind=kLoop, calls=%fused_computation.46 | loop fusion | flops 62720 | bytes 5632 | tf_op jit(solution)/shard_map/jit(remainder)/select_n | solution.py:59
  54.9 1.2 reduce-window.6
  56.1 0.2 slice_reduce_fusion
  56.4 0.1 bitcast_bitcast_fusion.1
  56.5 0.6 fusion.6
  57.1 0.4 select_reduce_fusion
  57.5 0.7 select_n.72
  58.2 11.5 %all-to-all-start = ((s32[32,1,56]{2,1,0:T(1,128)}), s32[32,1,56]{2,1,0:T(1,128)S(1)}, u32[]{:S(2)}, u32[]{:S(2)}) async-start(s32[32,1,56]{2,1,0:T(1,128)} %select_n.72), calls=%async_computation | async-start | bytes 32768 | tf_op jit(solution)/shard_map/all_to_all | solution.py:78
  69.7 0.7 convert_element_type.44
  70.4 4.6 %fusion = f32[448]{0:T(512)S(1)} fusion(bf16[448,8192]{1,0:T(8,128)(2,1)} %param.7), kind=kLoop, calls=%fused_computation.2 | loop fusion | flops 11009600 | bytes 7341824 | tf_op jit(solution)/shard_map/reduce_sum | solution.py:47
  75.1 5.5 %fusion.2 = bf16[448,8192]{1,0:T(8,128)(2,1)S(1)} fusion(bf16[448,8192]{1,0:T(8,128)(2,1)} %param.7, f32[8192]{0:T(1024)S(1)} %convert_element_type.44, f32[448]{0:T(512)S(1)} %add_rsqrt_fusion), kind=kLoop, calls=%fused_computation.4 | loop fusion | flops 14680064 | bytes 14714624 | tf_op jit(solution)/shard_map/convert_element_type | solution.py:48
  80.6 0.0 copy-start.1
  80.6 3.0 %copy-done.1 = bf16[448,8192]{1,0:T(8,128)(2,1)} copy-done((bf16[448,8192]{1,0:T(8,128)(2,1)}, bf16[448,8192]{1,0:T(8,128)(2,1)S(1)}, u32[]{:S(2)}) %copy-start.1) | copy-done | bytes 7340056
  83.6 4.1 %convolution_convert_fusion = bf16[1792,1024]{1,0:T(8,128)(2,1)} fusion(s32[448]{0:T(512)S(1)} %add_select_fusion.2, bf16[448,8192]{1,0:T(8,128)(2,1)S(1)} %fusion.2, s32[]{:T(128)S(6)} %select_n.73), kind=kOutput, calls=%fused_computation.8 | convolution fusion | flops 1646804992 | bytes 4589572 | tf_op jit(solution)/shard_map/dot_general | solution.py:70
  87.7 0.0 all-to-all-done
  87.7 9.9 %all-to-all-start.1 = ((bf16[32,56,1024]{2,1,0:T(8,128)(2,1)}), bf16[32,56,1024]{2,1,0:T(8,128)(2,1)}, u32[]{:S(2)}, u32[]{:S(2)}) async-start(bf16[32,56,1024]{2,1,0:T(8,128)(2,1)} %bitcast.121), calls=%async_computation.1 | async-start | bytes 7340032 | tf_op jit(solution)/shard_map/all_to_all | solution.py:77
  97.6 0.2 all-gather.3.cloned.1.call-start
  97.8 0.5 broadcast.414
  98.3 0.7 reduce.5
  99.0 0.1 eq.63
  99.2 83.8 %all-to-all-done.1 = bf16[32,56,1024]{2,1,0:T(8,128)(2,1)} async-done(((bf16[32,56,1024]{2,1,0:T(8,128)(2,1)}), bf16[32,56,1024]{2,1,0:T(8,128)(2,1)}, u32[]{:S(2)}, u32[]{:S(2)}) %all-to-all-start.1) | async-done | bytes 3670048 | tf_op jit(solution)/shard_map/all_to_all | solution.py:77
  183.0 0.0 copy-done
  183.0 4.2 %fusion.10 = f32[1792,128]{1,0:T(8,128)} fusion(bf16[1792,1024,1]{1,0,2:T(8,128)(2,1)} %bitcast.70, bf16[2,1024,128]{2,1,0:T(8,128)(2,1)S(1)} %copy-done, pred[1792,2]{0,1:T(4,128)(4,1)S(1)} %iota_compare_fusion.13), kind=kOutput, calls=%fused_computation.18 | convolution fusion | flops 940212224 | bytes 5115392 | tf_op jit(solution)/shard_map/rc,acm->ram/dot_general | solution.py:14
  187.1 0.0 all-gather.3.cloned.1.call-update
  187.2 43.7 %all-gather.3.cloned.1.call-done = f32[14336,128]{1,0:T(8,128)} async-done(((f32[1792,128]{1,0:T(8,128)}), f32[14336,128]{1,0:T(8,128)}) %all-gather.3.cloned.1.call-update) | async-done | bytes 7340048 | tf_op jit(solution)/shard_map/all_gather | solution.py:87
  230.8 0.0 copy-start.2
  230.8 3.5 %reduce_sum.49 = bf16[1792,128]{1,0:T(8,128)(2,1)S(1)} reduce(f32[8,1792,128]{2,1,0:T(8,128)} %bitcast.118, f32[]{:T(128)} %constant.46.clone.1), dimensions={0}, to_apply=%region_7.8 | reduce | flops 1605632 | bytes 7798788 | tf_op jit(solution)/shard_map/reduce_sum | solution.py:87
  234.4 0.2 copy.29
  234.6 0.0 copy-done.2
  234.6 0.5 fusion.7
  235.1 1.9 copy.31
  237.0 9.9 %all-to-all-start.2 = ((bf16[32,56,2,128]{3,2,1,0:T(2,128)(2,1)}), bf16[32,56,2,128]{3,2,1,0:T(2,128)(2,1)S(1)}, u32[]{:S(2)}, u32[]{:S(2)}) async-start(bf16[32,56,2,128]{3,2,1,0:T(2,128)(2,1)} %copy.31), calls=%async_computation.2 | async-start | bytes 1835008 | tf_op jit(solution)/shard_map/all_to_all | solution.py:91
  246.9 4.8 %copy.50 = bf16[1024,8,2,128]{3,1,2,0:T(8,128)(2,1)} copy(bf16[1024,8,2,128]{3,2,1,0:T(2,128)(2,1)} %bitcast.119) | data formatting | bytes 8388608
  251.7 6.4 %copy.26 = bf16[256,8192]{1,0:T(8,128)(2,1)} copy(bf16[256,8192]{0,1:T(8,128)(2,1)} %bitcast.117) | data formatting | bytes 8388608 | tf_op jit(solution)/shard_map/dot_general | solution.py:49
  258.1 15.1 %all-to-all-done.2 = bf16[32,56,2,128]{3,2,1,0:T(2,128)(2,1)S(1)} async-done(((bf16[32,56,2,128]{3,2,1,0:T(2,128)(2,1)}), bf16[32,56,2,128]{3,2,1,0:T(2,128)(2,1)S(1)}, u32[]{:S(2)}, u32[]{:S(2)}) %all-to-all-start.2) | async-done | bytes 917536 | tf_op jit(solution)/shard_map/all_to_all | solution.py:91
  273.2 0.7 fusion.17
  274.0 6.4 %fusion.18 = bf16[448,2,128]{2,0,1:T(8,128)(2,1)S(1)} fusion(bf16[2,128,8192]{2,1,0:T(8,128)(2,1)} %bitcast.120, bf16[448,8192]{1,0:T(8,128)(2,1)} %copy-done.1, f32[56,2,8,128]{3,2,1,0:T(8,128)S(1)} %fusion.17), kind=kOutput, calls=%fused_computation.24 | convolution fusion | flops 1879277568 | bytes 12222464 | tf_op jit(solution)/shard_map/dot_general | solution.py:49
  280.3 0.9 copy.33
  (10 shorter events, 0.1 us)
Async XLA Ops:
  6.5 176.5 %copy-start = (bf16[2,1024,128]{2,1,0:T(8,128)(2,1)S(1)}, bf16[2,1024,128]{2,1,0:T(8,128)(2,1)}, u32[]{:S(2)}) copy-start(bf16[2,1024,128]{2,1,0:T(8,128)(2,1)} %param.10) | copy-start | bytes 1572868
  58.2 29.5 %all-to-all-start = ((s32[32,1,56]{2,1,0:T(1,128)}), s32[32,1,56]{2,1,0:T(1,128)S(1)}, u32[]{:S(2)}, u32[]{:S(2)}) async-start(s32[32,1,56]{2,1,0:T(1,128)} %select_n.72), calls=%async_computation | async-start | bytes 32768 | tf_op jit(solution)/shard_map/all_to_all | solution.py:78
  80.6 3.0 %copy-start.1 = (bf16[448,8192]{1,0:T(8,128)(2,1)}, bf16[448,8192]{1,0:T(8,128)(2,1)S(1)}, u32[]{:S(2)}) copy-start(bf16[448,8192]{1,0:T(8,128)(2,1)S(1)} %fusion.2) | copy-start | bytes 22020100
  87.7 95.3 %all-to-all-start.1 = ((bf16[32,56,1024]{2,1,0:T(8,128)(2,1)}), bf16[32,56,1024]{2,1,0:T(8,128)(2,1)}, u32[]{:S(2)}, u32[]{:S(2)}) async-start(bf16[32,56,1024]{2,1,0:T(8,128)(2,1)} %bitcast.121), calls=%async_computation.1 | async-start | bytes 7340032 | tf_op jit(solution)/shard_map/all_to_all | solution.py:77
  97.6 133.2 %all-gather.3.cloned.1.call-start = ((), (), s32[]{:S(2)}) async-start(), calls=%async_computation.3 | async-start | bytes 8257536 | tf_op jit(solution)/shard_map/all_gather | solution.py:87
  230.8 3.7 %copy-start.2 = (bf16[2,2,64,128]{3,2,1,0:T(8,128)(2,1)S(1)}, bf16[2,2,64,128]{3,2,1,0:T(8,128)(2,1)}, u32[]{:S(2)}) copy-start(bf16[2,2,64,128]{3,2,1,0:T(8,128)(2,1)} %param.11) | copy-start | bytes 196612
  237.0 36.2 %all-to-all-start.2 = ((bf16[32,56,2,128]{3,2,1,0:T(2,128)(2,1)}), bf16[32,56,2,128]{3,2,1,0:T(2,128)(2,1)S(1)}, u32[]{:S(2)}, u32[]{:S(2)}) async-start(bf16[32,56,2,128]{3,2,1,0:T(2,128)(2,1)} %copy.31), calls=%async_computation.2 | async-start | bytes 1835008 | tf_op jit(solution)/shard_map/all_to_all | solution.py:91
Sparse Core Ops, SparseCore 0:
  187.3 43.5 all-gather.2
